TPU v7x, 32 devices: a whole 2x2x4 slice. The times are simulated.
32 devices in a mesh: row: 8 (over y, x, core), col: 4 (over z).
Axes of the slice: x: 2, y: 2, z: 4, core: 2. Of those that a mesh axis runs over, the one named last changes fastest.
Arguments:
- x_mat: float32 [512, 512], replicated, may hold values from -8 to 40, as said below
- y_inv: float32 [512, 512], replicated, may hold values from -8 to 40, as said below
- panel_blocks: bfloat16 [512, 4096], replicated, may hold values from -6 to 6
- panel_pos: int32 [512], replicated, may hold values from 0 to 63
- group_blocks: int32 [32, 2], replicated, may hold values from 0 to 63
- cons_blocks: bfloat16 [57344, 4096], P(('row', 'col')), may hold values from -6 to 6
- slot_block: int32 [57344], P(('row', 'col')), may hold values from 0 to 1
- slot_row: int32 [57344], P(('row', 'col')), may hold values from 0 to 32767, as said below
- group_size: int32 [32], P(('row', 'col')), may hold values from 768 to 1792, as said below
- trailing: float32 [32768, 2048], P('row', 'col'), may hold values from -6 to 6
Outputs:
- lower_panel: float32 [32768, 512], P(('row', 'col'))
- updated: float32 [32768, 2048], P('row', 'col')
Inputs may be any that keep to these rules, and one draw needn't show every extreme that they name: `x_mat`: symmetric positive definite. `y_inv`: symmetric positive definite. `slot_row`: over all groups, the live slots hold every row 0 to 32767 exactly once; the live slots of one group hold at most 56 rows of one aligned range of 1024 rows, and that most is reached in every draw; other slots hold arbitrary rows. `group_size`: the live slots of a group are its first slots; some group has exactly 1792 in every draw.
All inputs are finite; a program needn't handle non-finite values.
Results may differ from a plain program's by a relative error of at most 0.004.
Values may be sent and summed in bfloat16 or wider, within the bound.
A program may use at most 192 MiB of HBM per device.

v0:
```python
import math

import jax
import jax.numpy as jnp
from jax import lax
from jax.sharding import PartitionSpec as P


def build_h(values, position, x_mat, y_inv):
    highest = lax.Precision.HIGHEST
    matrix_order = x_mat.shape[0]
    block_size = math.isqrt(values.shape[0])
    block_count = matrix_order // block_size
    e_mat = values.reshape(block_size, block_size).astype(jnp.float32)
    row_start = position // block_count * block_size
    col_start = position % block_count * block_size
    x_left = lax.dynamic_slice_in_dim(x_mat, row_start, block_size, 1)
    x_right = lax.dynamic_slice_in_dim(x_mat, col_start, block_size, 1)
    y_low = lax.dynamic_slice_in_dim(y_inv, col_start, block_size, 0)
    y_high = lax.dynamic_slice_in_dim(y_inv, row_start, block_size, 0)
    term_one = jnp.dot(jnp.dot(x_left, e_mat, precision=highest), y_low, precision=highest)
    term_two = jnp.dot(jnp.dot(x_right, e_mat.T, precision=highest), y_high, precision=highest)
    g_mat = term_one + term_two
    h_mat = (g_mat + g_mat.T).astype(jnp.bfloat16)
    h_mat = h_mat.reshape(block_count, block_size, block_count, block_size).transpose(0, 2, 1, 3)
    return h_mat.reshape(block_count * block_count, block_size * block_size)


def body(
    x_mat,
    y_inv,
    panel_blocks,
    panel_pos,
    group_blocks,
    cons_blocks,
    slot_block,
    slot_row,
    group_size,
    trailing,
):
    rows_size = lax.axis_size("row")
    cols_size = lax.axis_size("col")
    devices = rows_size * cols_size
    col_index = lax.axis_index("col")
    device_id = lax.axis_index("row") * cols_size + col_index
    panel_cols = panel_blocks.shape[0]
    per_device = panel_cols // devices
    own_values = lax.dynamic_slice_in_dim(panel_blocks, device_id * per_device, per_device, 0)
    own_pos = lax.dynamic_slice_in_dim(panel_pos, device_id * per_device, per_device, 0)
    own_blocks = jax.vmap(build_h, in_axes=(0, 0, None, None))(own_values, own_pos, x_mat, y_inv)
    chosen = jnp.take(own_blocks, panel_pos, axis=1)
    column_part = jnp.einsum("if,nif->in", panel_blocks, chosen, preferred_element_type=jnp.float32)
    panel_schur = lax.all_gather(column_part, ("row", "col"), axis=1, tiled=True)
    symmetric = 0.5 * (panel_schur + panel_schur.T)
    diag_shift = 0.01 * jnp.mean(jnp.diagonal(symmetric))
    factor = jnp.linalg.cholesky(symmetric + diag_shift * jnp.eye(panel_cols, dtype=jnp.float32))
    slot_count = cons_blocks.shape[0]
    outgoing = jnp.take(own_blocks, group_blocks.T, axis=1)
    received = lax.all_to_all(outgoing, ("row", "col"), split_axis=2, concat_axis=2, tiled=True)
    running = jnp.zeros((slot_count, received.shape[2], received.shape[0]), jnp.float32)
    for slot_index in range(received.shape[1]):
        product_part = jnp.einsum(
            "sf,ndf->sdn", cons_blocks, received[:, slot_index], preferred_element_type=jnp.float32
        )
        running = jnp.where((slot_block == slot_index)[:, None, None], product_part, running)
    schur_rows = running.reshape(slot_count, panel_cols)
    sub_rows = trailing.shape[0] // cols_size
    base_share = sub_rows // devices
    spread = sub_rows - devices // 4 * base_share
    capacity = base_share + (spread + devices - 1) // devices
    live_slots = jnp.arange(slot_count, dtype=jnp.int32) < group_size[0]
    target = slot_row // sub_rows
    dest_hits = (
        (target[:, None] == jnp.arange(devices, dtype=jnp.int32)[None, :]) & live_slots[:, None]
    ).astype(jnp.int32)
    before = jnp.cumsum(dest_hits, axis=0) - dest_hits
    dest_rank = jnp.sum(before * dest_hits, axis=1)
    slot_place = jnp.where(live_slots, target * capacity + dest_rank, devices * capacity)
    send_rows = (
        jnp.zeros((devices * capacity, panel_cols), jnp.float32)
        .at[slot_place]
        .set(schur_rows, mode="drop")
    )
    send_local = (
        jnp.full((devices * capacity,), sub_rows, jnp.int32)
        .at[slot_place]
        .set(slot_row % sub_rows, mode="drop")
    )
    recv_rows, recv_local = (
        lax.all_to_all(
            send_rows.reshape(devices, capacity, panel_cols),
            ("row", "col"),
            split_axis=0,
            concat_axis=0,
            tiled=True,
        ),
        lax.all_to_all(
            send_local.reshape(devices, capacity),
            ("row", "col"),
            split_axis=0,
            concat_axis=0,
            tiled=True,
        ),
    )
    row_slab = (
        jnp.zeros((sub_rows, panel_cols), jnp.float32)
        .at[recv_local.reshape(-1)]
        .set(recv_rows.reshape(-1, panel_cols), mode="drop")
    )
    lower_slab = lax.linalg.triangular_solve(
        factor, row_slab, left_side=False, lower=True, transpose_a=True
    )
    all_rows = lax.all_gather(lower_slab, "col", axis=0, tiled=True)
    block_rows = trailing.shape[1] // rows_size
    own_rows = lax.dynamic_slice_in_dim(all_rows, col_index * block_rows, block_rows, 0)
    picked = lax.all_gather(own_rows, "row", axis=0, tiled=True)
    updated = trailing - jnp.dot(all_rows, picked.T, precision=lax.Precision.HIGHEST)
    return (lower_slab, updated)


def solution(mesh):
    return jax.shard_map(
        body,
        mesh=mesh,
        in_specs=(
            P(),
            P(),
            P(),
            P(),
            P(),
            P(("row", "col"), None),
            P(("row", "col")),
            P(("row", "col")),
            P(("row", "col")),
            P("row", "col"),
        ),
        out_specs=(P(("row", "col"), None), P("row", "col")),
        check_vma=False,
    )
```

profile of v0, /device:TPU:0, one launch (start us, length us, event | category | flops | bytes accessed | tf_op | source)
XLA Modules:
  0.0 992.5 jit_solution(9979744026841548414)
XLA Ops:
  10.2 2.5 broadcast.301.clone
  12.6 31.8 %while.5 = (s32[]{:T(128)}, f32[512,512]{1,0:T(8,128)S(1)}, s32[16,2]{0,1:T(2,128)S(1)}, f32[16,512,64]{2,1,0:T(8,128)}, s32[]{:T(128)}) while((s32[]{:T(128)}, f32[512,512]{1,0:T(8,128)S(1)}, s32[16,2]{0,1:T(2,128)S(1)}, f32[16,512,64]{2,1,0:T(8,128)}, s32[]{:T(128)}) %tuple.108), condition=%wide.while_cond, body=%wide.while_body.sunk | while | flops 2 | bytes 394329 | solution.py:17
  45.8 34.9 %while.6 = (s32[]{:T(128)}, f32[512,512]{1,0:T(8,128)}, s32[16,2]{0,1:T(2,128)S(1)}, f32[16,64,512]{2,1,0:T(8,128)S(1)}, s32[]{:T(128)}) while((s32[]{:T(128)}, f32[512,512]{1,0:T(8,128)}, s32[16,2]{0,1:T(2,128)S(1)}, f32[16,64,512]{2,1,0:T(8,128)S(1)}, s32[]{:T(128)}) %tuple.90), condition=%wide.while_cond.1, body=%wide.while_body.1.sunk | while | flops 2 | bytes 262241 | solution.py:19
  80.8 2.6 broadcast.301.clone.1
  83.4 35.3 %while.7 = (s32[]{:T(128)}, f32[512,512]{1,0:T(8,128)S(1)}, s32[16,2]{0,1:T(2,128)S(1)}, f32[16,512,64]{2,1,0:T(8,128)}, s32[]{:T(128)}) while((s32[]{:T(128)}, f32[512,512]{1,0:T(8,128)S(1)}, s32[16,2]{0,1:T(2,128)S(1)}, f32[16,512,64]{2,1,0:T(8,128)}, s32[]{:T(128)}) %tuple.109), condition=%wide.while_cond.2, body=%wide.while_body.2.sunk | while | flops 2 | bytes 394329 | solution.py:18
  118.7 5.0 fusion.71
  123.8 4.1 fusion.73
  129.4 47.0 %while.8 = (s32[]{:T(128)}, f32[512,512]{1,0:T(8,128)}, s32[16,2]{0,1:T(2,128)S(1)}, f32[16,64,512]{2,1,0:T(8,128)}, s32[]{:T(128)}) while((s32[]{:T(128)}, f32[512,512]{1,0:T(8,128)}, s32[16,2]{0,1:T(2,128)S(1)}, f32[16,64,512]{2,1,0:T(8,128)}, s32[]{:T(128)}) %tuple.110), condition=%wide.while_cond.3, body=%wide.while_body.3.sunk | while | flops 2 | bytes 263257 | solution.py:20
  130.1 2.3 bitcast_dynamic-update-slice_fusion.13
  133.0 2.3 bitcast_dynamic-update-slice_fusion.13
  136.0 2.3 bitcast_dynamic-update-slice_fusion.13
  138.9 2.3 bitcast_dynamic-update-slice_fusion.13
  141.8 2.3 bitcast_dynamic-update-slice_fusion.13
  144.8 2.3 bitcast_dynamic-update-slice_fusion.13
  147.7 2.3 bitcast_dynamic-update-slice_fusion.13
  150.6 2.3 bitcast_dynamic-update-slice_fusion.13
  153.6 2.3 bitcast_dynamic-update-slice_fusion.13
  156.5 2.3 bitcast_dynamic-update-slice_fusion.13
  159.5 2.3 bitcast_dynamic-update-slice_fusion.13
  162.4 2.3 bitcast_dynamic-update-slice_fusion.13
  165.3 2.3 bitcast_dynamic-update-slice_fusion.13
  168.3 2.3 bitcast_dynamic-update-slice_fusion.13
  171.2 2.3 bitcast_dynamic-update-slice_fusion.13
  174.1 2.3 bitcast_dynamic-update-slice_fusion.13
  176.4 17.1 %fusion.72 = f32[16,512,512]{2,1,0:T(8,128)} fusion(f32[16,512,64]{1,2,0:T(8,128)S(1)} %fusion.71, f32[16,64,512]{2,1,0:T(8,128)} %copy-done.3), kind=kOutput, calls=%fused_computation.160 | convolution fusion | flops 3221225472 | bytes 20971520 | tf_op jit(solution)/shard_map/vmap()/dot_general | solution.py:21
  193.5 18.9 %convolution_add_fusion = f32[16,512,512]{2,1,0:T(8,128)} fusion(f32[16,512,512]{2,1,0:T(8,128)} %fusion.72, f32[16,512,64]{1,2,0:T(8,128)S(1)} %copy-done.2, f32[16,64,512]{2,1,0:T(8,128)S(1)} %copy-done.4), kind=kOutput, calls=%fused_computation.28 | convolution fusion | flops 3225419776 | bytes 37748736 | tf_op jit(solution)/shard_map/vmap()/dot_general | solution.py:22
  212.4 17.6 %copy.62 = f32[16,512,512]{1,2,0:T(8,128)} copy(f32[16,512,512]{2,1,0:T(8,128)} %convolution_add_fusion) | data formatting | bytes 33554432 | tf_op jit(solution)/shard_map/vmap()/add | solution.py:23
  230.0 15.1 %fusion.5 = bf16[16,512,512]{2,1,0:T(8,128)(2,1)} fusion(f32[16,512,512]{2,1,0:T(8,128)} %convolution_add_fusion, f32[16,512,512]{1,2,0:T(8,128)} %copy.62), kind=kLoop, calls=%fused_computation.22 | loop fusion | flops 8388608 | bytes 41943040 | tf_op jit(solution)/shard_map/vmap()/convert_element_type | solution.py:24
  245.0 21.2 %reshape.134 = bf16[16,8,64,8,64]{4,3,2,1,0:T(8,128)(2,1)} reshape(bf16[16,512,512]{2,1,0:T(8,128)(2,1)} %fusion.5) | data formatting | bytes 16777216 | tf_op jit(solution)/shard_map/vmap()/reshape | solution.py:25
  266.3 15.1 %copy.93 = bf16[16,8,64,8,64]{4,2,3,1,0:T(8,128)(2,1)} copy(bf16[16,8,64,8,64]{4,3,2,1,0:T(8,128)(2,1)} %reshape.134) | data formatting | bytes 16777216 | tf_op jit(solution)/shard_map/vmap()/reshape | solution.py:25
  281.3 22.6 %reshape.135 = bf16[16,64,4096]{2,1,0:T(8,128)(2,1)} reshape(bf16[16,8,8,64,64]{4,3,2,1,0:T(8,128)(2,1)} %bitcast.160) | data formatting | bytes 16777216 | tf_op jit(solution)/shard_map/vmap()/reshape | solution.py:26
  303.9 11.2 %copy.64 = bf16[16,64,4096]{2,0,1:T(8,128)(2,1)} copy(bf16[16,64,4096]{2,1,0:T(8,128)(2,1)} %reshape.135) | data formatting | bytes 16777216 | tf_op jit(solution)/shard_map/vmap()/reshape | solution.py:26
  315.2 9.6 gather_fusion
  324.7 7.6 select_bitcast_fusion
  332.4 7.8 copy.65
  340.1 7.4 all-to-all-start.1
  347.7 28.5 %gather_fusion.1 = bf16[512,16,4096]{2,1,0:T(8,128)(2,1)} fusion(bf16[16,64,4096]{2,0,1:T(8,128)(2,1)} %copy.64, s32[1024]{0:T(1024)S(1)} %pad_clamp_fusion), kind=kCustom, calls=%fused_computation.1 | custom fusion | bytes 134219776 | tf_op jit(solution)/shard_map/jit(_take)/gather | solution.py:51
  376.2 30.4 %fusion = f32[512,1,16]{2,1,0:T(1,128)S(1)} fusion(bf16[512,16,4096]{2,1,0:T(8,128)(2,1)} %gather_fusion.1, pred[512]{0:T(512)(128)(4,1)S(1)} %compare_and_fusion, bf16[512,4096,1]{1,0,2:T(8,128)(2,1)} %bitcast.170), kind=kOutput, calls=%fused_computation.16 | convolution fusion | flops 100663296 | bytes 71336448 | tf_op jit(solution)/shard_map/if,nif->in/dot_general | solution.py:52
  408.1 9.1 reduce-window.6
  417.9 7.1 scatter_custom_fusion
  425.7 108.3 %all-to-all-done.1 = bf16[16,2,32,4096]{3,0,1,2:T(8,128)(2,1)} async-done(((bf16[16,2,32,4096]{3,0,1,2:T(8,128)(2,1)}), bf16[16,2,32,4096]{3,0,1,2:T(8,128)(2,1)}, u32[]{:S(2)}, u32[]{:S(2)}) %all-to-all-start.1) | async-done | bytes 8388640 | tf_op jit(solution)/shard_map/all_to_all | solution.py:59
  534.0 8.5 all-to-all-start
  542.6 5.2 fusion.68
  547.8 15.2 %fusion.6 = f32[16,32,1792]{2,1,0:T(8,128)} fusion(bf16[1792,4096]{1,0:T(8,128)(2,1)} %param.15, bf16[16,1,32,4096]{3,0,1,2:T(8,128)(2,1)S(1)} %get-tuple-element.97), kind=kOutput, calls=%fused_computation.24 | convolution fusion | flops 7516192768 | bytes 22544384 | tf_op jit(solution)/shard_map/sf,ndf->sdn/dot_general | solution.py:62
  563.0 18.1 %select_bitcast_fusion.1 = f32[1792,32,16]{0,1,2:T(8,128)} fusion(f32[16,32,1792]{2,1,0:T(8,128)} %fusion.6, bf16[1792,4096]{1,0:T(8,128)(2,1)} %param.15, bf16[16,1,32,4096]{3,0,1,2:T(8,128)(2,1)} %get-tuple-element.96, pred[1792]{0:T(1024)(128)(4,1)S(1)} %get-tuple-element.109, pred[1792]{0:T(1024)(128)(4,1)S(1)} %get-tuple-element.108), kind=kOutput, calls=%fused_computation.34 | convolution fusion | flops 7518027776 | bytes 26217984 | tf_op jit(solution)/shard_map/sf,ndf->sdn/dot_general | solution.py:62
  581.1 6.0 copy.68
  587.1 5.1 copy.69
  592.2 13.1 %scatter_custom_fusion.1 = f32[1792,512]{1,0:T(8,128)} fusion(s32[1792]{0:T(1024)S(1)} %compare_select_fusion.1, f32[1792,512]{1,0:T(8,128)} %copy.69, f32[]{:T(128)} %constant.245.clone.1), kind=kCustom, calls=%fused_computation.36 | custom fusion | bytes 3670528 | tf_op jit(solution)/shard_map/scatter | solution.py:82
  605.4 6.1 all-to-all-start.2
  615.8 4.9 gather_fusion.2
  622.6 11.7 %cholesky.103 = f32[128,128]{1,0:T(8,128)S(1)} custom-call(f32[128,128]{1,0:T(8,128)S(1)} %cholesky.263), custom_call_target="Cholesky" | custom-call | tf_op jit(solution)/shard_map/jit(cholesky)/cholesky | solution.py:56
  634.5 9.8 custom-call.30
  645.0 11.7 %cholesky.215 = f32[128,128]{1,0:T(8,128)S(1)} custom-call(f32[128,128]{1,0:T(8,128)S(1)} %cholesky.267), custom_call_target="Cholesky" | custom-call | tf_op jit(solution)/shard_map/jit(cholesky)/cholesky | solution.py:56
  656.7 10.0 %custom-call.31 = f32[1,128,128]{1,2,0:T(8,128)S(1)} custom-call(f32[1,128,128]{2,1,0:T(8,128)S(1)} %get-tuple-element.104), custom_call_target="InvertDiagBlocksLowerTriangular" | custom-call | tf_op jit(solution)/shard_map/jit(cholesky)/cholesky | solution.py:56
  667.4 11.7 %cholesky.236 = f32[128,128]{1,0:T(8,128)S(1)} custom-call(f32[128,128]{1,0:T(8,128)S(1)} %cholesky.272), custom_call_target="Cholesky" | custom-call | tf_op jit(solution)/shard_map/jit(cholesky)/cholesky | solution.py:56
  679.1 9.8 custom-call.32
  689.5 11.7 %cholesky.253 = f32[128,128]{1,0:T(8,128)S(1)} custom-call(f32[128,128]{1,0:T(8,128)S(1)} %convolution_subtract_fusion.5), custom_call_target="Cholesky" | custom-call | tf_op jit(solution)/shard_map/jit(cholesky)/cholesky | solution.py:56
  706.7 10.6 %while.9 = (s32[]{:T(128)}, f32[512,512]{1,0:T(8,128)S(1)}, s32[4,2]{0,1:T(2,128)S(1)}, f32[4,128,128]{2,1,0:T(8,128)}, s32[]{:T(128)}) while((s32[]{:T(128)}, f32[512,512]{1,0:T(8,128)S(1)}, s32[4,2]{0,1:T(2,128)S(1)}, f32[4,128,128]{2,1,0:T(8,128)}, s32[]{:T(128)}) %tuple.99), condition=%wide.while_cond.4, body=%wide.while_body.4.sunk | while | flops 2 | bytes 132705 | solution.py:110
  717.2 40.1 %custom-call.33 = f32[4,128,128]{1,2,0:T(8,128)S(1)} custom-call(f32[4,128,128]{2,1,0:T(8,128)} %get-tuple-element.41), custom_call_target="InvertDiagBlocksLowerTriangular" | custom-call | tf_op jit(solution)/shard_map/triangular_solve | solution.py:110
  757.4 11.6 %scatter_custom_fusion.2 = f32[1024,512]{1,0:T(8,128)S(1)} fusion(s32[1792]{0:T(1024)S(1)} %fusion.57, f32[1792,512]{1,0:T(8,128)} %bitcast.17, f32[]{:T(128)} %constant.245.clone.1), kind=kCustom, calls=%fused_computation.63 | custom fusion | bytes 2097664 | tf_op jit(solution)/shard_map/scatter | solution.py:108
  773.7 2.8 fusion.21
  779.0 150.6 %all-gather.6.cloned.1.call-done = f32[4096,512]{0,1:T(8,128)} async-done(((f32[1024,512]{0,1:T(8,128)}), f32[4096,512]{0,1:T(8,128)}) %all-gather.6.cloned.1.call-update) | async-done | bytes 8388624 | tf_op jit(solution)/shard_map/all_gather | solution.py:113
  933.4 20.4 %all-gather.8.cloned.1.call-done = f32[512,512]{1,0:T(8,128)} async-done(((f32[64,512]{1,0:T(8,128)}), f32[512,512]{1,0:T(8,128)}) %all-gather.8.cloned.1.call-update) | async-done | bytes 1048592 | tf_op jit(solution)/shard_map/all_gather | solution.py:116
  953.7 31.8 %convolution_subtract_fusion = f32[4096,512]{1,0:T(8,128)} fusion(f32[4096,512]{1,0:T(8,128)} %param.19, f32[4096,512]{0,1:T(8,128)} %all-gather.6.cloned.1.call-done, f32[512,512]{1,0:T(8,128)} %all-gather.8.cloned.1.call-done), kind=kOutput, calls=%fused_computation.31 | convolution fusion | flops 12886999040 | bytes 26214400 | tf_op jit(solution)/shard_map/dot_general | solution.py:117
  (286 shorter events, 152.6 us)
Async XLA Ops:
  7.2 5.5 copy-start.5
  80.8 38.0 %copy-start.3 = (f32[16,64,512]{2,1,0:T(8,128)}, f32[16,64,512]{2,1,0:T(8,128)S(1)}, u32[]{:S(2)}) copy-start(f32[16,64,512]{2,1,0:T(8,128)S(1)} %get-tuple-element.17) | copy-start | bytes 6291460
  118.7 5.0 copy-start.1
  176.4 17.1 %copy-start.2 = (f32[16,512,64]{1,2,0:T(8,128)S(1)}, f32[16,512,64]{1,2,0:T(8,128)}, u32[]{:S(2)}) copy-start(f32[16,512,64]{1,2,0:T(8,128)} %fusion.73) | copy-start | bytes 6291460
  176.4 17.1 %copy-start.4 = (f32[16,64,512]{2,1,0:T(8,128)S(1)}, f32[16,64,512]{2,1,0:T(8,128)}, u32[]{:S(2)}) copy-start(f32[16,64,512]{2,1,0:T(8,128)} %get-tuple-element.33) | copy-start | bytes 6291460
  340.1 7.5 copy-start.6
  340.1 193.9 %all-to-all-start.1 = ((bf16[16,2,32,4096]{3,0,1,2:T(8,128)(2,1)}), bf16[16,2,32,4096]{3,0,1,2:T(8,128)(2,1)}, u32[]{:S(2)}, u32[]{:S(2)}) async-start(bf16[16,2,32,4096]{3,0,1,2:T(8,128)(2,1)} %copy.65), calls=%async_computation.1 | async-start | bytes 16777216 | tf_op jit(solution)/shard_map/all_to_all | solution.py:59
  347.6 265.2 %all-gather.4.cloned.1.call-start = ((), (), s32[]{:S(2)}) async-start(), calls=%async_computation.3 | async-start | bytes 1081344 | tf_op jit(solution)/shard_map/all_gather | solution.py:53
  376.2 31.8 %copy-start.7 = (s32[1792]{0:T(1024)S(1)}, s32[1792]{0:T(1024)}, u32[]{:S(2)}) copy-start(s32[1792]{0:T(1024)} %param.17) | copy-start | bytes 21508
  376.2 49.5 %copy-start.8 = (s32[1792]{0:T(1024)S(1)}, s32[1792]{0:T(1024)}, u32[]{:S(2)}) copy-start(s32[1792]{0:T(1024)} %param.16) | copy-start | bytes 21508
  534.0 71.3 %all-to-all-start = ((s32[32,1,56]{2,1,0:T(1,128)}), s32[32,1,56]{2,1,0:T(1,128)S(1)}, u32[]{:S(2)}, u32[]{:S(2)}) async-start(s32[32,1,56]{2,1,0:T(1,128)} %all_to_all.12), calls=%async_computation | async-start | bytes 32768 | tf_op jit(solution)/shard_map/all_to_all | solution.py:97
  605.4 152.0 %all-to-all-start.2 = ((f32[32,56,512]{2,1,0:T(8,128)}), f32[32,56,512]{2,1,0:T(8,128)}, u32[]{:S(2)}, u32[]{:S(2)}) async-start(f32[32,56,512]{2,1,0:T(8,128)} %bitcast.164), calls=%async_computation.2 | async-start | bytes 7340032 | tf_op jit(solution)/shard_map/all_to_all | solution.py:90
  611.4 318.2 %all-gather.6.cloned.1.call-start = ((), (), s32[]{:S(2)}) async-start(), calls=%async_computation.4 | async-start | bytes 10485760 | tf_op jit(solution)/shard_map/all_gather | solution.py:113
  778.7 152.8 %copy-start = (f32[1024,512]{0,1:T(8,128)S(1)}, f32[1024,512]{0,1:T(8,128)}, u32[]{:S(2)}) copy-start(f32[1024,512]{0,1:T(8,128)} %pad_maximum_fusion) | copy-start | bytes 6291460
  778.7 175.0 %all-gather.8.cloned.1.call-start = ((), (), s32[]{:S(2)}) async-start(), calls=%async_computation.5 | async-start | bytes 1179648 | tf_op jit(solution)/shard_map/all_gather | solution.py:116
Sparse Core Ops, SparseCore 0:
  407.5 96.1 all-gather.3
  778.9 150.7 all-gather.5
  932.1 21.5 all-gather.7
where the time goes:
time: 1000 us; the launch traced here: 993 us
  local copies, waits for them, and re-layouts  362 us (36%)
  waiting for transfers between devices  279 us (28%)
  other arithmetic  159 us (16%)
  matrix products  151 us (15%)
  starting transfers between devices  22.4 us (2%)
  between operations  18.5 us (2%)
    all_gather x1, waiting for transfers between devices, body(): all_rows = lax.all_gather(lower_slab, 'col', axis=0, tiled=True)  151 us
    gather x192, local copies, waits for them, and re-layouts  149 us
    all_to_all x1, waiting for transfers between devices, body(): lax.all_to_all(outgoing, ('row', 'col'), split_axis=2, concat_axis=2, til...  108 us
    another operation x15, other arithmetic, body(): jnp.linalg.cholesky(symmetric + diag_shift * jnp.eye(panel_cols, dtype=jn...  79.2 us
    another operation x4, other arithmetic, body(): lax.linalg.triangular_solve(factor, row_slab, left_side=False, lower=True...  41.8 us
    reshape x2, local copies, waits for them, and re-layouts, build_h(): h_mat.reshape(block_count, block_size, block_count, block_size)  36.3 us
    reshape x2, local copies, waits for them, and re-layouts, build_h(): return h_mat.reshape(block_count * block_count, block_size * block_size)  33.7 us
    dot_general x2, matrix products, body(): jnp.einsum('sf,ndf->sdn', cons_blocks, received[:, slot_index], preferred...  33.3 us
  transfers between devices with their start and end apart: 6, of which 3 were waited for; matrix products, arithmetic and copies ran while one was open for 29% of the time, Pallas kernels for 0%

commit v1 on v0

v1 whole, which is shorter than its diff:
```python
import functools
import math

import jax
import jax.numpy as jnp
from jax import lax
from jax.experimental import pallas as pl
from jax.experimental.pallas import tpu as pltpu
from jax.sharding import PartitionSpec as P

BF16 = jnp.bfloat16
F32 = jnp.float32


def split(value):
    high = value.astype(BF16)
    low = (value - high.astype(F32)).astype(BF16)
    return high, low


def halves(block_size, rows):
    return lax.broadcasted_iota(jnp.int32, (rows, 2 * block_size), 1) < block_size


def congruence(p, q, pair, left_ref, high_ref, low_ref):
    block_size = pair.shape[0]
    keep = halves(block_size, block_size)
    zero = jnp.zeros_like(pair)
    first = jnp.where(keep, pair, zero)
    second = jnp.where(keep, zero, pair)
    stacked = jnp.concatenate([first, first, second, second], axis=0)
    left = jnp.concatenate([left_ref[p], left_ref[q]], axis=1)
    inner = jnp.dot(left, stacked, preferred_element_type=F32)
    rows = inner.shape[0] // 2
    wide = jnp.concatenate([inner[:rows], inner[rows:]], axis=1)
    wide_high, wide_low = split(wide)
    z_high = jnp.concatenate([high_ref[0, q], high_ref[0, p], high_ref[1, q], high_ref[1, p]], axis=0)
    z_low = jnp.concatenate([low_ref[0, q], low_ref[0, p], low_ref[1, q], low_ref[1, p]], axis=0)
    dot = functools.partial(jnp.dot, preferred_element_type=F32)
    return dot(wide_high, z_high) + (dot(wide_high, z_low) + dot(wide_low, z_high))


def own_kernel(block_count, pos_ref, pair_ref, left_ref, high_ref, low_ref, out_ref, scr):
    step = pl.program_id(0)
    position = pos_ref[step]
    p = position // block_count
    q = position % block_count
    h = congruence(p, q, pair_ref[0], left_ref, high_ref, low_ref)
    order = h.shape[0]
    block_size = order // block_count
    lanes = 2 * block_size
    groups = order // lanes
    for g in range(groups):
        scr[g * order : (g + 1) * order, :] = h[:, g * lanes : (g + 1) * lanes]
    keep = halves(block_size, block_count)
    for g in range(groups):
        for r in range(0, block_size, 2):
            even = scr[pl.ds(g * order + r, block_count, stride=block_size), :]
            odd = scr[pl.ds(g * order + r + 1, block_count, stride=block_size), :]
            one = jnp.where(keep, even, pltpu.roll(odd, block_size, 1))
            two = jnp.where(keep, pltpu.roll(even, block_size, 1), odd)
            both = jnp.concatenate([one, two], axis=0).astype(BF16)
            out_ref[
                2 * g * block_count : 2 * (g + 1) * block_count,
                r * block_size : (r + 2) * block_size,
            ] = both


def group_kernel(block_count, tile, pos_ref, pair_ref, left_ref, high_ref, low_ref, out_ref, scr):
    step = pl.program_id(0)
    block_size = pair_ref.shape[1]
    keep_rows = halves(block_size, block_size)
    for j in range(tile):
        position = pos_ref[step * tile + j]
        p = position // block_count
        q = position % block_count
        h = congruence(p, q, pair_ref[j], left_ref, high_ref, low_ref)
        scr[j * block_size : (j + 1) * block_size, :] = jnp.where(
            keep_rows, h[:block_size], h[block_size:]
        )
    keep = halves(block_size, tile)
    for r in range(0, block_size, 2):
        even = scr[pl.ds(r, tile, stride=block_size), :]
        odd = scr[pl.ds(r + 1, tile, stride=block_size), :]
        columns = slice(r * block_size, (r + 2) * block_size)
        out_ref[0, :, columns] = jnp.where(keep, even, pltpu.roll(odd, block_size, 1)).astype(BF16)
        out_ref[1, :, columns] = jnp.where(keep, pltpu.roll(even, block_size, 1), odd).astype(BF16)


def whole(shape):
    return pl.BlockSpec(shape, lambda *_: (0,) * len(shape))


def own_table(pairs, positions, left, high, low, block_count):
    count, block_size, lanes = pairs.shape
    order = block_count * block_size
    rows = block_count * block_count
    return pl.pallas_call(
        functools.partial(own_kernel, block_count),
        grid_spec=pltpu.PrefetchScalarGridSpec(
            num_scalar_prefetch=1,
            grid=(count,),
            in_specs=[
                pl.BlockSpec((1, block_size, lanes), lambda i, _: (i, 0, 0)),
                whole(left.shape),
                whole(high.shape),
                whole(low.shape),
            ],
            out_specs=pl.BlockSpec((rows, block_size * block_size), lambda i, _: (i, 0)),
            scratch_shapes=[pltpu.VMEM((order * order // lanes, lanes), F32)],
        ),
        out_shape=jax.ShapeDtypeStruct((count * rows, block_size * block_size), BF16),
        name="own_table",
    )(positions, pairs, left, high, low)


def group_table(pairs, positions, left, high, low, block_count):
    count, block_size, lanes = pairs.shape
    tile = 16
    return pl.pallas_call(
        functools.partial(group_kernel, block_count, tile),
        grid_spec=pltpu.PrefetchScalarGridSpec(
            num_scalar_prefetch=1,
            grid=(count // tile,),
            in_specs=[
                pl.BlockSpec((tile, block_size, lanes), lambda i, _: (i, 0, 0)),
                whole(left.shape),
                whole(high.shape),
                whole(low.shape),
            ],
            out_specs=pl.BlockSpec((2, tile, block_size * block_size), lambda i, _: (0, i, 0)),
            scratch_shapes=[pltpu.VMEM((tile * block_size, lanes), F32)],
        ),
        out_shape=jax.ShapeDtypeStruct((2, count, block_size * block_size), BF16),
        cost_estimate=pl.CostEstimate(
            flops=40 * 10**9, bytes_accessed=20 * 10**6, transcendentals=0
        ),
        name="group_table",
    )(positions, pairs, left, high, low)


def hdot(a, b, contract):
    return lax.dot_general(
        a, b, ((contract[:1], contract[1:]), ((), ())),
        precision=lax.Precision.HIGHEST, preferred_element_type=F32,
    )


def factor_kernel(block, s_ref, out_ref, a, work):
    order = s_ref.shape[0]
    count = order // block
    groups = block // 8
    a[...] = s_ref[...]
    row_id = lax.broadcasted_iota(jnp.int32, (8, 1), 0)
    eye = (
        lax.broadcasted_iota(jnp.int32, (block, block), 0)
        == lax.broadcasted_iota(jnp.int32, (block, block), 1)
    ).astype(F32)

    def diagonal(b, carry):
        start = pl.multiple_of(b * block, block)
        work[:, :block] = a[pl.ds(start, block), pl.ds(start, block)]
        work[:, block:] = eye
        rows = [work[8 * g : 8 * g + 8, :] for g in range(groups)]
        for k in range(block):
            g, s = divmod(k, 8)
            pivot_row = rows[g][s : s + 1, :]
            d = pivot_row[:, k : k + 1]
            inv = lax.rsqrt(d)
            inv = inv * (1.5 - 0.5 * d * inv * inv)
            scaled = pivot_row * inv
            for i in range(g, groups):
                mult = rows[i][:, k : k + 1] * inv
                if i == g:
                    mult = jnp.where(row_id > s, mult, 0.0)
                    rows[i] = jnp.where(row_id == s, scaled, rows[i] - mult * scaled)
                else:
                    rows[i] = rows[i] - mult * scaled
        inverse = jnp.concatenate([row[:, block:] for row in rows], axis=0)
        out_ref[pl.ds(start, block), pl.ds(start, block)] = inverse
        panel = hdot(a[:, pl.ds(start, block)], inverse, (1, 1))
        below = lax.broadcasted_iota(jnp.int32, (order, 1), 0) >= start + block
        panel = jnp.where(below, panel, 0.0)
        a[:, pl.ds(start, block)] = panel
        return carry, panel

    def body(b, carry):
        _, panel = diagonal(b, carry)
        start = pl.multiple_of(b * block, block)

        for i in range(1, count):
            @pl.when(b < i)
            def _():
                piece = a[i * block : (i + 1) * block, pl.ds(start, block)]
                cols = slice(i * block, (i + 1) * block)
                a[:, cols] = a[:, cols] - hdot(panel, piece, (1, 1))

        return carry

    lax.fori_loop(0, count, body, 0)
    for i in range(count):
        for b in range(i + 1, count):
            out_ref[i * block : (i + 1) * block, b * block : (b + 1) * block] = jnp.zeros(
                (block, block), F32
            )
    for i in range(1, count):
        low_row = a[i * block : (i + 1) * block, : i * block]
        total = hdot(low_row, out_ref[: i * block, : i * block], (1, 0))
        own = out_ref[i * block : (i + 1) * block, i * block : (i + 1) * block]
        out_ref[i * block : (i + 1) * block, : i * block] = -hdot(own, total, (1, 0))


def inverse_factor(matrix):
    order = matrix.shape[0]
    block = 128
    return pl.pallas_call(
        functools.partial(factor_kernel, block),
        in_specs=[pl.BlockSpec(memory_space=pltpu.VMEM)],
        out_specs=pl.BlockSpec(memory_space=pltpu.VMEM),
        out_shape=jax.ShapeDtypeStruct((order, order), F32),
        scratch_shapes=[pltpu.VMEM((order, order), F32), pltpu.VMEM((block, 2 * block), F32)],
        cost_estimate=pl.CostEstimate(
            flops=60 * 10**9, bytes_accessed=2 * 10**6, transcendentals=order
        ),
        name="inverse_factor",
    )(matrix)


def blocks_of_columns(matrix, block_count):
    rows = matrix.shape[0]
    return matrix.reshape(rows, block_count, -1).transpose(1, 0, 2)


def body(
    x_mat,
    y_inv,
    panel_blocks,
    panel_pos,
    group_blocks,
    cons_blocks,
    slot_block,
    slot_row,
    group_size,
    trailing,
):
    rows_size = lax.axis_size("row")
    cols_size = lax.axis_size("col")
    devices = rows_size * cols_size
    col_index = lax.axis_index("col")
    device_id = lax.axis_index("row") * cols_size + col_index
    panel_cols = panel_blocks.shape[0]
    per_device = panel_cols // devices
    order = x_mat.shape[0]
    block_size = math.isqrt(panel_blocks.shape[1])
    block_count = order // block_size
    square = panel_blocks.reshape(panel_cols, block_size, block_size)
    pairs = jnp.concatenate([square, square.transpose(0, 2, 1)], axis=2)
    both = jnp.stack([y_inv, x_mat])
    rounded = lax.reduce_precision(both, exponent_bits=8, mantissa_bits=7)
    both_high = rounded.astype(BF16)
    both_low = lax.reduce_precision(both - rounded, exponent_bits=8, mantissa_bits=7).astype(BF16)
    high = both_high.reshape(2, block_count, block_size, order)
    low = both_low.reshape(2, block_count, block_size, order)
    tall_high = jnp.concatenate([both_high[1], both_high[0]], axis=0)
    tall_low = jnp.concatenate([both_low[1], both_low[0]], axis=0)
    left = jnp.concatenate(
        [blocks_of_columns(tall_high, block_count), blocks_of_columns(tall_low, block_count)], axis=2
    )
    own_pairs = lax.dynamic_slice_in_dim(pairs, device_id * per_device, per_device, 0)
    own_pos = lax.dynamic_slice_in_dim(panel_pos, device_id * per_device, per_device, 0)
    own_rows = own_table(own_pairs, own_pos, left, high, low, block_count)
    products = lax.dot_general(
        own_rows, panel_blocks, (((1,), (1,)), ((), ())), preferred_element_type=F32
    )
    place = panel_pos % block_count * block_count + panel_pos // block_count
    position_count = block_count * block_count
    hit = jnp.arange(position_count, dtype=jnp.int32)[:, None] == place[None, :]
    row_part = jnp.sum(
        jnp.where(hit[None], products.reshape(per_device, position_count, panel_cols), 0.0), axis=1
    )
    panel_schur = lax.all_gather(row_part, ("row", "col"), axis=0, tiled=True)

    own_group = lax.dynamic_index_in_dim(group_blocks, device_id, 0, keepdims=False)
    slots = own_group.shape[0]
    lefts, highs, lows = [], [], []
    for slot_index in range(slots):
        a_block = own_group[slot_index] // block_count
        b_start = own_group[slot_index] % block_count * block_size
        lefts.append(
            lax.dynamic_slice_in_dim(
                left.reshape(block_count, 2, order, 2 * block_size), a_block * block_size, block_size, 2
            )
        )
        highs.append(lax.dynamic_slice_in_dim(high, b_start, block_size, 3))
        lows.append(lax.dynamic_slice_in_dim(low, b_start, block_size, 3))
    group_left = jnp.concatenate(lefts, axis=2).reshape(
        block_count, 2 * slots * block_size, 2 * block_size
    )
    group_rows = group_table(
        pairs, panel_pos, group_left, jnp.concatenate(highs, axis=3), jnp.concatenate(lows, axis=3),
        block_count,
    )
    slot_count = cons_blocks.shape[0]
    running = None
    for slot_index in range(slots):
        product_part = lax.dot_general(
            cons_blocks, group_rows[slot_index], (((1,), (1,)), ((), ())), preferred_element_type=F32
        )
        if running is None:
            running = jnp.where((slot_block == slot_index)[:, None], product_part, 0.0)
        else:
            running = jnp.where((slot_block == slot_index)[:, None], product_part, running)
    schur_rows = running

    sub_rows = trailing.shape[0] // cols_size
    base_share = sub_rows // devices
    spread = sub_rows - devices // 4 * base_share
    capacity = base_share + (spread + devices - 1) // devices
    live_slots = jnp.arange(slot_count, dtype=jnp.int32) < group_size[0]
    target = slot_row // sub_rows
    dest_hits = (
        (target[:, None] == jnp.arange(devices, dtype=jnp.int32)[None, :]) & live_slots[:, None]
    ).astype(jnp.int32)
    before = jnp.cumsum(dest_hits, axis=0) - dest_hits
    dest_rank = jnp.sum(before * dest_hits, axis=1)
    slot_place = jnp.where(live_slots, target * capacity + dest_rank, devices * capacity)
    place_ids = jnp.arange(devices * capacity, dtype=jnp.int32)
    send_hits = (place_ids[:, None] == slot_place[None, :]).astype(BF16)
    send_rows = jnp.dot(
        send_hits, schur_rows.astype(BF16), preferred_element_type=F32
    ).astype(BF16)
    send_local = (
        jnp.full((devices * capacity,), sub_rows, jnp.int32)
        .at[slot_place]
        .set(slot_row % sub_rows, mode="drop")
    )
    exchange = functools.partial(
        lax.all_to_all, axis_name=("row", "col"), split_axis=0, concat_axis=0, tiled=True
    )
    recv_local = exchange(send_local.reshape(devices, capacity))
    recv_rows = exchange(send_rows.reshape(devices, capacity, panel_cols))
    symmetric = 0.5 * (panel_schur + panel_schur.T)
    diag_shift = 0.01 * jnp.mean(jnp.diagonal(symmetric))
    inverse = inverse_factor(symmetric + diag_shift * jnp.eye(panel_cols, dtype=F32))
    local_ids = jnp.arange(sub_rows, dtype=jnp.int32)
    recv_hits = (local_ids[:, None] == recv_local.reshape(1, -1)).astype(BF16)
    row_slab = jnp.dot(
        recv_hits, recv_rows.reshape(-1, panel_cols), preferred_element_type=F32
    )
    lower_slab = hdot(row_slab, inverse, (1, 1))
    all_rows = lax.all_gather(lower_slab.astype(BF16), "col", axis=0, tiled=True)
    block_rows = trailing.shape[1] // rows_size
    own_rows = lax.dynamic_slice_in_dim(all_rows, col_index * block_rows, block_rows, 0)
    picked = lax.all_gather(own_rows, "row", axis=0, tiled=True)
    update = lax.dot_general(
        all_rows, picked, (((1,), (1,)), ((), ())), preferred_element_type=F32
    )
    return (lower_slab, trailing - update)


def solution(mesh):
    return jax.shard_map(
        body,
        mesh=mesh,
        in_specs=(
            P(),
            P(),
            P(),
            P(),
            P(),
            P(("row", "col"), None),
            P(("row", "col")),
            P(("row", "col")),
            P(("row", "col")),
            P("row", "col"),
        ),
        out_specs=(P(("row", "col"), None), P("row", "col")),
        check_vma=False,
    )
```

time: 1000 us -> 521 us (0.52)
  local copies, waits for them, and re-layouts: 362 us -> 66.6 us
  Pallas kernels: 0 us -> 224 us
  waiting for transfers between devices: 279 us -> 82.1 us
  other arithmetic: 159 us -> 35.5 us
  matrix products: 151 us -> 61.1 us
    pallas_call x0 -> x3, Pallas kernels: none -> 224 us  [the longest x1 139 us: group_table(): pl.pallas_call(functools.partial(group_kernel, block_count, tile), grid_s...]
    gather x194 -> x0, local copies, waits for them, and re-layouts: 187 us -> none
    another operation x22 -> x3, other arithmetic: 130 us -> 9.25 us  [the longest x15 79.2 us: body(): jnp.linalg.cholesky(symmetric + diag_shift * jnp.eye(panel_cols, dtype=jn...]
    all_to_all x3 -> x2, waiting for transfers between devices: 108 us -> 0.01 us  [the longest x1 0.01 us: body(): recv_rows = exchange(send_rows.reshape(devices, capacity, panel_cols))]
    all_gather x3 -> x2, waiting for transfers between devices: 171 us -> 82.1 us  [the longest x1 82.1 us: body(): lax.all_gather(lower_slab.astype(BF16), 'col', axis=0, tiled=True)]
    dot_general x8 -> x6, matrix products: 141 us -> 61.1 us  [the longest x1 18.8 us: body(): jnp.dot(send_hits, schur_rows.astype(BF16), preferred_element_type=F32)]
    reshape x7 -> x2, local copies, waits for them, and re-layouts: 75.5 us -> 28.7 us  [body(): square = panel_blocks.reshape(panel_cols, block_size, block_size)]
    scatter x2 -> x0, local copies, waits for them, and re-layouts: 24.8 us -> none  [the longest x1 13.1 us: body(): send_rows = jnp.zeros((devices * capacity, panel_cols), jnp.float32).at[s...]
  transfers between devices with their start and end apart: 6 -> 4, of which waited for: 3 -> 1; matrix products, arithmetic and copies ran while one was open for 29% -> 15% of each run, Pallas kernels for 0% -> 38%
where the time goes in v1:
time: 521 us; the launch traced here: 513 us
  Pallas kernels  224 us (43%)
  waiting for transfers between devices  82.1 us (16%)
  local copies, waits for them, and re-layouts  66.6 us (13%)
  matrix products  61.1 us (12%)
  other arithmetic  35.5 us (7%)
  between operations  20.7 us (4%)
  starting transfers between devices  14 us (3%)
  blocking collectives  9.8 us (2%)
    pallas_call x1, Pallas kernels, group_table(): pl.pallas_call(functools.partial(group_kernel, block_count, tile), grid_s...  139 us
    all_gather x1, waiting for transfers between devices, body(): lax.all_gather(lower_slab.astype(BF16), 'col', axis=0, tiled=True)  82.1 us
    pallas_call x1, Pallas kernels, inverse_factor(): pl.pallas_call(functools.partial(factor_kernel, block), in_specs=[pl.Bloc...  55.1 us
    pallas_call x1, Pallas kernels, own_table(): pl.pallas_call(functools.partial(own_kernel, block_count), grid_spec=pltp...  29.1 us
    reshape x2, local copies, waits for them, and re-layouts, body(): square = panel_blocks.reshape(panel_cols, block_size, block_size)  28.7 us
    dot_general x1, matrix products, body(): jnp.dot(send_hits, schur_rows.astype(BF16), preferred_element_type=F32)  18.8 us
    dot_general x1, matrix products, body(): lax.dot_general(cons_blocks, group_rows[slot_index], (((1,), (1,)), ((),...  13.4 us
    concatenate x2, other arithmetic, body(): pairs = jnp.concatenate([square, square.transpose(0, 2, 1)], axis=2)  13 us
  transfers between devices with their start and end apart: 4, of which 1 were waited for; matrix products, arithmetic and copies ran while one was open for 15% of the time, Pallas kernels for 38%

profile of v1, /device:TPU:0, one launch (start us, length us, event | category | flops | bytes accessed | tf_op | source)
XLA Modules:
  0.0 513.4 jit_solution(11813711501293940192)
XLA Ops:
  7.2 0.0 copy-start
  7.2 0.0 all-gather.3.cloned.1.call-start
  7.2 6.5 %copy.28 = bf16[512,4096]{0,1:T(8,128)(2,1)} copy(bf16[512,4096]{1,0:T(8,128)(2,1)} %param.12) | data formatting | bytes 8388608 | tf_op args[2]
  13.7 15.6 %copy.29 = bf16[512,64,64]{1,2,0:T(8,128)(2,1)} copy(bf16[512,64,64]{0,2,1:T(8,128)(2,1)} %bitcast.74) | data formatting | bytes 8388608 | tf_op jit(solution)/shard_map/reshape | solution.py:256
  29.3 13.1 %copy.30 = bf16[512,64,64]{2,1,0:T(8,128)(2,1)} copy(bf16[512,64,64]{0,2,1:T(8,128)(2,1)} %bitcast.75) | data formatting | bytes 8388608 | tf_op jit(solution)/shard_map/reshape | solution.py:256
  42.5 0.6 dynamic_slice.38.pos_ref
  43.1 0.3 copy.31
  43.4 1.3 copy.32
  44.7 1.6 reduce-precision_convert_fusion.1
  46.3 1.3 fusion.31
  47.7 1.5 copy.33
  49.2 2.5 copy.34
  51.7 2.3 copy.35
  54.0 2.4 copy.36
  56.4 2.0 fusion.15.pair_ref
  58.4 0.4 maximum_bitcast_fusion
  58.8 0.8 copy-done.7
  59.6 0.3 copy-done.8
  59.9 0.4 maximum_bitcast_fusion.1
  60.3 2.5 pad_maximum_fusion.2.left_ref
  62.8 1.8 fusion.10
  64.6 29.1 %own_table.1 = bf16[1024,4096]{1,0:T(8,128)(2,1)} custom-call(s32[16]{0:T(128)} %dynamic_slice.38.pos_ref, bf16[16,64,128]{2,1,0:T(8,128)(2,1)} %fusion.15.pair_ref, bf16[8,1024,128]{2,1,0:T(8,128)(2,1)} %pad_maximum_fusion.2.left_ref, bf16[2,8,64,512]{3,2,1,0:T(8,128)(2,1)} %get-tuple-element.5.high_ref, bf16[2,8,64,512]{3,2,1,0:T(8,128)(2,1)} %get-tuple-element.4.low_ref), custom_call_target="tpu_custom_call" | custom-call | tf_op jit(solution)/shard_map/own_table/pallas_call | solution.py:98
  93.7 0.0 copy-start.10
  93.7 9.7 %select_reduce_fusion = f32[16,512]{1,0:T(8,128)} fusion(pred[64,512]{1,0:T(8,128)(4,1)S(1)} %iota_compare_fusion.9, bf16[1024,4096]{1,0:T(8,128)(2,1)} %own_table.1, bf16[512,4096]{1,0:T(8,128)(2,1)} %param.12), kind=kOutput, calls=%fused_computation.31 | convolution fusion | flops 4296007680 | bytes 12648448 | tf_op jit(solution)/shard_map/dot_general | solution.py:272
  103.4 0.0 all-gather.3.cloned.1.call-update
  104.2 9.1 %reduce-window.6 = s32[32,14,128]{2,1,0:T(8,128)S(1)} reduce-window(s32[32,14,128]{2,1,0:T(8,128)S(1)} %fusion.17, s32[]{:T(128)} %constant.112.clone.1), window={size=1x1x128 pad=0_0x0_0x127_0}, to_apply=%region_0.1 | reduce-window | flops 7282688 | bytes 458756 | tf_op jit(solution)/shard_map/reduce-window
  113.3 0.1 slice.46
  113.4 0.2 copy.26
  113.6 0.1 copy.27
  113.7 0.1 broadcast_add_fusion
  113.9 0.1 fusion.20
  114.0 7.1 %scatter_custom_fusion = s32[1792]{0:T(1024)S(1)} fusion(s32[1792]{0:T(1024)S(1)} %get-tuple-element.2, s32[1792]{0:T(1024)S(1)} %get-tuple-element.18, s32[]{:T(128)} %constant.110.clone.1), kind=kCustom, calls=%fused_computation.68 | custom fusion | bytes 7172 | tf_op jit(solution)/shard_map/scatter | solution.py:335
  121.1 0.7 all_to_all.9
  121.8 7.8 %all-to-all-start = ((s32[32,1,56]{2,1,0:T(1,128)}), s32[32,1,56]{2,1,0:T(1,128)S(1)}, u32[]{:S(2)}, u32[]{:S(2)}) async-start(s32[32,1,56]{2,1,0:T(1,128)} %all_to_all.9), calls=%async_computation | async-start | bytes 32768 | tf_op jit(solution)/shard_map/all_to_all | solution.py:340
  129.7 0.1 constant_dynamic-slice_fusion.7
  129.8 0.6 fusion.33
  135.2 11.0 %pad_maximum_fusion.pair_ref = bf16[512,64,128]{2,1,0:T(8,128)(2,1)} fusion(bf16[512,64,64]{2,1,0:T(8,128)(2,1)} %bitcast.73, bf16[512,64,64]{2,1,0:T(8,128)(2,1)} %copy.30), kind=kLoop, calls=%fused_computation.5 | loop fusion | flops 16777216 | bytes 16777216 | tf_op jit(solution)/shard_map/concatenate | solution.py:257
  146.2 1.1 constant_dynamic-slice_fusion.6
  147.3 0.8 pad_maximum_fusion.4
  148.2 0.4 constant_dynamic-slice_fusion.2
  148.6 0.9 pad_maximum_fusion.5.high_ref
  149.4 0.9 pad_maximum_fusion.6.low_ref
  150.3 139.4 %group_table.1 = bf16[2,512,4096]{2,1,0:T(8,128)(2,1)} custom-call(s32[512]{0:T(512)} %pos_ref.1, bf16[512,64,128]{2,1,0:T(8,128)(2,1)} %pad_maximum_fusion.pair_ref, bf16[8,256,128]{2,1,0:T(8,128)(2,1)} %bitcast.87, bf16[2,8,64,128]{3,2,1,0:T(8,128)(2,1)} %pad_maximum_fusion.5.high_ref, bf16[2,8,64,128]{3,2,1,0:T(8,128)(2,1)} %pad_maximum_fusion.6.low_ref), custom_call_target="tpu_custom_call" | custom-call | flops 40000000000 | bytes 20000000 | tf_op jit(solution)/shard_map/group_table/pallas_call | solution.py:120
  289.7 13.4 %fusion.3 = bf16[512,1792]{1,0:T(8,128)(2,1)S(1)} fusion(bf16[1792,4096]{1,0:T(8,128)(2,1)} %param.15, bf16[2,512,4096]{2,1,0:T(8,128)(2,1)} %group_table.1), kind=kOutput, calls=%fused_computation.12 | convolution fusion | flops 7516192768 | bytes 20709376 | tf_op jit(solution)/shard_map/dot_general | solution.py:306
  303.0 18.8 %fusion.6 = bf16[1792,512]{1,0:T(8,128)(2,1)} fusion(bf16[512,1792]{1,0:T(8,128)(2,1)S(1)} %fusion.3, bf16[1792,4096]{1,0:T(8,128)(2,1)} %param.15, bf16[2,512,4096]{2,1,0:T(8,128)(2,1)} %group_table.1, s32[1792]{0:T(1024)S(1)} %get-tuple-element.3, pred[1792]{0:T(1024)(128)(4,1)S(1)} %get-tuple-element.21, pred[1792]{0:T(1024)(128)(4,1)S(1)} %get-tuple-element.20), kind=kOutput, calls=%fused_computation.21 | convolution fusion | flops 10810490880 | bytes 22555136 | tf_op jit(solution)/shard_map/dot_general | solution.py:329
  321.9 6.0 %all-to-all-start.1 = ((bf16[32,56,512]{2,1,0:T(8,128)(2,1)}), bf16[32,56,512]{2,1,0:T(8,128)(2,1)}, u32[]{:S(2)}, u32[]{:S(2)}) async-start(bf16[32,56,512]{2,1,0:T(8,128)(2,1)} %bitcast.22), calls=%async_computation.1 | async-start | bytes 3670016 | tf_op jit(solution)/shard_map/all_to_all | solution.py:341
  328.0 0.0 all-gather.5.cloned.1.call-start
  328.0 0.5 broadcast.121
  328.5 0.7 reduce.3
  329.2 0.1 eq.93
  329.3 0.0 all-gather.3.cloned.1.call-done
  329.3 1.6 copy.37
  330.9 1.5 fusion.14
  332.4 4.5 gather_fusion
  336.9 0.6 reduce_sum.29
  338.2 1.1 select_add_fusion.s_ref
  339.2 55.1 %inverse_factor.1 = f32[512,512]{1,0:T(8,128)} custom-call(f32[512,512]{1,0:T(8,128)} %select_add_fusion.s_ref), custom_call_target="tpu_custom_call" | custom-call | flops 60000002048 | bytes 2000000 | tf_op jit(solution)/shard_map/inverse_factor/pallas_call | solution.py:216
  394.3 3.6 fusion.1
  398.0 5.1 fusion.34
  403.1 0.0 all-gather.5.cloned.1.call-update
  403.2 82.1 %all-gather.5.cloned.1.call-done = bf16[4096,512]{1,0:T(8,128)(2,1)} async-done(((bf16[1024,512]{1,0:T(8,128)(2,1)}), bf16[4096,512]{1,0:T(8,128)(2,1)}) %all-gather.5.cloned.1.call-update) | async-done | bytes 4194320 | tf_op jit(solution)/shard_map/all_gather | solution.py:351
  485.2 0.8 constant_dynamic-slice_fusion
  486.1 9.8 %all_gather.11 = bf16[512,512]{1,0:T(8,128)(2,1)S(1)} all-gather(bf16[64,512]{1,0:T(8,128)(2,1)S(1)} %constant_dynamic-slice_fusion), channel_id=1, replica_groups=mesh['row'=8,'col'=4] {'row'}, dimensions={0}, use_global_device_ids=true | all-gather | bytes 589824 | tf_op jit(solution)/shard_map/all_gather | solution.py:354
  495.9 10.4 %convolution_subtract_fusion = f32[4096,512]{1,0:T(8,128)} fusion(f32[4096,512]{1,0:T(8,128)} %param.19, bf16[4096,512]{1,0:T(8,128)(2,1)} %all-gather.5.cloned.1.call-done, bf16[512,512]{1,0:T(8,128)(2,1)S(1)} %all_gather.11), kind=kOutput, calls=%fused_computation.10 | convolution fusion | flops 2149580800 | bytes 21495808 | tf_op jit(solution)/shard_map/dot_general | solution.py:355
  (34 shorter events, 0.2 us)
Async XLA Ops:
  7.2 122.5 %copy-start = (s32[32,2]{0,1:T(2,128)S(1)}, s32[32,2]{0,1:T(2,128)}, u32[]{:S(2)}) copy-start(s32[32,2]{0,1:T(2,128)} %param.14) | copy-start | bytes 772
  7.2 322.1 %all-gather.3.cloned.1.call-start = ((), (), s32[]{:S(2)}) async-start(), calls=%async_computation.2 | async-start | bytes 1081344 | tf_op jit(solution)/shard_map/all_gather | solution.py:281
  29.3 13.1 %copy-start.12 = (s32[512]{0:T(512)S(1)}, s32[512]{0:T(512)}, u32[]{:S(2)}) copy-start(s32[512]{0:T(512)} %pos_ref.1) | copy-start | bytes 6148
  29.3 13.8 %copy-start.5 = (f32[512,512]{1,0:T(8,128)S(1)}, f32[512,512]{1,0:T(8,128)}, u32[]{:S(2)}) copy-start(f32[512,512]{1,0:T(8,128)} %param.11) | copy-start | bytes 3145732
  29.3 14.1 %copy-start.4 = (f32[512,512]{1,0:T(8,128)S(1)}, f32[512,512]{1,0:T(8,128)}, u32[]{:S(2)}) copy-start(f32[512,512]{1,0:T(8,128)} %param.10) | copy-start | bytes 3145732
  56.4 2.0 copy-start.6
  58.4 1.2 copy-start.7
  58.4 1.5 copy-start.8
  93.7 9.8 %copy-start.10 = (s32[1792]{0:T(1024)S(1)}, s32[1792]{0:T(1024)}, u32[]{:S(2)}) copy-start(s32[1792]{0:T(1024)} %param.17) | copy-start | bytes 21508
  121.8 200.1 %all-to-all-start = ((s32[32,1,56]{2,1,0:T(1,128)}), s32[32,1,56]{2,1,0:T(1,128)S(1)}, u32[]{:S(2)}, u32[]{:S(2)}) async-start(s32[32,1,56]{2,1,0:T(1,128)} %all_to_all.9), calls=%async_computation | async-start | bytes 32768 | tf_op jit(solution)/shard_map/all_to_all | solution.py:340
  135.1 11.0 %copy-start.11 = (s32[1792]{0:T(1024)S(1)}, s32[1792]{0:T(1024)}, u32[]{:S(2)}) copy-start(s32[1792]{0:T(1024)} %param.16) | copy-start | bytes 21508
  135.1 13.0 %copy-start.2 = (bf16[2,8,64,512]{3,2,1,0:T(8,128)(2,1)S(1)}, bf16[2,8,64,512]{3,2,1,0:T(8,128)(2,1)}, u32[]{:S(2)}) copy-start(bf16[2,8,64,512]{3,2,1,0:T(8,128)(2,1)} %get-tuple-element.4.low_ref) | copy-start | bytes 3145732
  135.1 13.0 %copy-start.3 = (bf16[2,8,64,512]{3,2,1,0:T(8,128)(2,1)S(1)}, bf16[2,8,64,512]{3,2,1,0:T(8,128)(2,1)}, u32[]{:S(2)}) copy-start(bf16[2,8,64,512]{3,2,1,0:T(8,128)(2,1)} %get-tuple-element.5.high_ref) | copy-start | bytes 3145732
  321.9 72.4 %all-to-all-start.1 = ((bf16[32,56,512]{2,1,0:T(8,128)(2,1)}), bf16[32,56,512]{2,1,0:T(8,128)(2,1)}, u32[]{:S(2)}, u32[]{:S(2)}) async-start(bf16[32,56,512]{2,1,0:T(8,128)(2,1)} %bitcast.22), calls=%async_computation.1 | async-start | bytes 3670016 | tf_op jit(solution)/shard_map/all_to_all | solution.py:341
  328.0 157.3 %all-gather.5.cloned.1.call-start = ((), (), s32[]{:S(2)}) async-start(), calls=%async_computation.3 | async-start | bytes 5242880 | tf_op jit(solution)/shard_map/all_gather | solution.py:351
  394.3 3.7 copy-start.9
  495.9 10.5 %copy-start.1 = (s32[32,2]{0,1:T(2,128)S(1)}, s32[32,2]{0,1:T(2,128)}, u32[]{:S(2)}) copy-start(s32[32,2]{0,1:T(2,128)} %param.14) | copy-start | bytes 772
Sparse Core Ops, SparseCore 0:
  103.6 56.5 all-gather.2
  403.3 81.9 all-gather.4
